TPU v7x, 128 devices: a whole 4x4x4 slice. The times are simulated.
128 devices in a mesh: ctx: 8 (over x, y_lo), ffn: 16 (over z, y_hi, core).
Axes of the slice: x: 4, y: 4 (y_hi: 2, y_lo: 2; y = y_hi * 2 + y_lo), z: 4, core: 2. Of those that a mesh axis runs over, the one named last changes fastest.
Arguments:
- resid_in: bfloat16 [1024, 4096], P(('ctx', 'ffn')), may hold values from -6 to 6
- queries: bfloat16 [1024, 4096], P('ctx', 'ffn'), may hold values from -6 to 6
- keys_in: bfloat16 [1024, 1024], P('ctx'), may hold values from -6 to 6
- value_rows_input: bfloat16 [1024, 1024], P('ctx'), may hold values from -6 to 6
- w_out: bfloat16 [4096, 4096], P('ffn'), may hold values from -0.09375 to 0.09375
- norm_gain: float32 [4096], replicated, may hold values from 0.5 to 1.5
- w_gate: bfloat16 [4096, 7168], P(None, 'ffn'), may hold values from -0.09375 to 0.09375
- w_up: bfloat16 [4096, 7168], P(None, 'ffn'), may hold values from -0.09375 to 0.09375
- w_down: bfloat16 [7168, 4096], P('ffn'), may hold values from -0.0625 to 0.0625
- cotangent: bfloat16 [1024, 4096], P(('ctx', 'ffn')), may hold values from -6 to 6
- positions: int32 [1024], P('ctx'), may hold values from 0 to 1023, as said below
- doc_ids: int32 [1024], replicated, may hold values from 0 to 3, never falling along the last dimension, each value on 1 to 512 neighbouring positions
Outputs:
- mixed: bfloat16 [1024, 4096], P(('ctx', 'ffn'))
- grad_resid: bfloat16 [1024, 4096], P(('ctx', 'ffn'))
- grad_queries: bfloat16 [1024, 4096], P('ctx', 'ffn')
- key_gradient_rows: float32 [1024, 1024], P(('ctx', 'ffn'))
- value_gradient_rows: float32 [1024, 1024], P(('ctx', 'ffn'))
- grad_gain: float32 [4096], replicated
- grad_w_out: float32 [4096, 4096], P('ffn', 'ctx')
- grad_w_gate: float32 [4096, 7168], P('ctx', 'ffn')
- grad_w_up: float32 [4096, 7168], P('ctx', 'ffn')
- grad_w_down: float32 [7168, 4096], P('ffn', 'ctx')
Inputs may be any that keep to these rules, and one draw needn't show every extreme that they name: Each aligned block of 64 rows holds 64 consecutive positions in rising order, and every position occurs once.
All inputs are finite; a program needn't handle non-finite values.
Results may differ from a plain program's by a relative error of at most 0.033.
Values may be sent and summed in bfloat16 or wider, within the bound.
A program may use at most 128 MiB of HBM per device.

v0:
```python
import math
import jax
import jax.numpy as jnp
from jax import lax
from jax.sharding import PartitionSpec as P

QUERY_HEADS = 32
KEY_VALUE_HEADS = 8
HEAD_WIDTH = 128
masked_fill = -1e30
norm_eps = 1e-05


def passed_along(value, axis, by):
    count = lax.axis_size(axis)
    return lax.ppermute(value, axis, [(i, (i + by) % count) for i in range(count)])


def tile_visible(query_pos, query_seg, key_pos, key_seg):
    return (key_pos[None, :] <= query_pos[:, None]) & (key_seg[None, :] == query_seg[:, None])


def forward_tile(folded, q_heads, key_piece, value_piece, visible, score_scale):
    row_max, row_total, accumulated = folded
    scores = (
        jnp.einsum("rhd,kd->hrk", q_heads, key_piece, preferred_element_type=jnp.float32)
        * score_scale
    )
    scores = jnp.where(visible[None], scores, masked_fill)
    new_max = jnp.maximum(row_max, jnp.max(scores, axis=2))
    weights = jnp.where(visible[None], jnp.exp(scores - new_max[:, :, None]), 0.0)
    shrink = jnp.exp(row_max - new_max)
    new_total = row_total * shrink + jnp.sum(weights, axis=2)
    product = jnp.einsum(
        "hrk,kd->hrd", weights.astype(jnp.bfloat16), value_piece, preferred_element_type=jnp.float32
    )
    return (new_max, new_total, accumulated * shrink[:, :, None] + product)


def row_contract(left_rows, right_rows):
    return jnp.einsum("rd,rf->df", left_rows, right_rows, preferred_element_type=jnp.float32)


def body(
    resid_in,
    queries,
    keys_in,
    value_rows_input,
    w_out,
    norm_gain,
    w_gate,
    w_up,
    w_down,
    cotangent,
    positions,
    doc_ids,
):
    row_count = queries.shape[0]
    resident_heads = queries.shape[1] // HEAD_WIDTH
    ctx_size = lax.axis_size("ctx")
    ctx_index = lax.axis_index("ctx")
    key_value_group = lax.axis_index("ffn") * resident_heads // (QUERY_HEADS // KEY_VALUE_HEADS)
    score_scale = 1.0 / math.sqrt(HEAD_WIDTH)
    all_pos = lax.all_gather(positions, "ctx", axis=0, tiled=True)
    all_seg = doc_ids[all_pos]
    own_seg = doc_ids[positions]
    key_own = lax.dynamic_slice_in_dim(keys_in, key_value_group * HEAD_WIDTH, HEAD_WIDTH, 1)
    value_own = lax.dynamic_slice_in_dim(
        value_rows_input, key_value_group * HEAD_WIDTH, HEAD_WIDTH, 1
    )
    kv_pair = jnp.stack((key_own, value_own), axis=1)
    q_heads = queries.reshape(row_count, resident_heads, HEAD_WIDTH)

    def key_visible(row_start, row_num):
        return tile_visible(
            positions,
            own_seg,
            lax.dynamic_slice_in_dim(all_pos, row_start, row_num, 0),
            lax.dynamic_slice_in_dim(all_seg, row_start, row_num, 0),
        )

    def fold_keys(folded, shard_rows, row_start):
        visible = key_visible(row_start, shard_rows.shape[0])
        return forward_tile(
            folded, q_heads, shard_rows[:, 0], shard_rows[:, 1], visible, score_scale
        )

    start_state = (
        jnp.full((resident_heads, row_count), masked_fill, jnp.float32),
        jnp.zeros((resident_heads, row_count), jnp.float32),
        jnp.zeros((resident_heads, row_count, HEAD_WIDTH), jnp.float32),
    )

    def pass_step(turn_index, running):
        folded, travel = running
        travel = passed_along(travel, "ctx", 1)
        source = (ctx_index - turn_index - 1) % ctx_size
        return (fold_keys(folded, travel, source * row_count), travel)

    first_state = fold_keys(start_state, kv_pair, ctx_index * row_count)
    (row_max, row_total, accumulated), unused = lax.fori_loop(
        0, ctx_size - 1, pass_step, (first_state, kv_pair)
    )
    attended = (accumulated / row_total[:, :, None]).astype(jnp.bfloat16)
    log_totals = row_max + jnp.log(row_total)
    attended_rows = jnp.transpose(attended, (1, 0, 2)).reshape(
        row_count, resident_heads * HEAD_WIDTH
    )
    projected = lax.psum_scatter(
        jnp.dot(attended_rows, w_out, preferred_element_type=jnp.float32).astype(jnp.bfloat16),
        "ffn",
        scatter_dimension=0,
        tiled=True,
    ).astype(jnp.float32)
    hidden_bf = (resid_in.astype(jnp.float32) + projected).astype(jnp.bfloat16)
    hidden_f = lax.optimization_barrier(hidden_bf).astype(jnp.float32)
    inv_rms = lax.rsqrt(jnp.mean(hidden_f * hidden_f, axis=1, keepdims=True) + norm_eps)
    normed = (hidden_f * inv_rms * norm_gain).astype(jnp.bfloat16)
    normed_rows = lax.all_gather(normed, "ffn", axis=0, tiled=True)
    gate_pre = jnp.dot(normed_rows, w_gate, preferred_element_type=jnp.float32)
    up_proj = jnp.dot(normed_rows, w_up, preferred_element_type=jnp.float32)
    gate_sig = jax.nn.sigmoid(gate_pre)
    activated = (gate_pre * gate_sig * up_proj).astype(jnp.bfloat16)
    mixed = (
        hidden_f
        + lax.psum_scatter(
            jnp.dot(activated, w_down, preferred_element_type=jnp.float32).astype(jnp.bfloat16),
            "ffn",
            scatter_dimension=0,
            tiled=True,
        ).astype(jnp.float32)
    ).astype(jnp.bfloat16)
    cot_rows = lax.all_gather(cotangent, "ffn", axis=0, tiled=True)
    grad_act = jnp.dot(cot_rows, w_down.T, preferred_element_type=jnp.float32)
    grad_up = (grad_act * gate_pre * gate_sig).astype(jnp.bfloat16)
    grad_gate = (grad_act * up_proj * gate_sig * (1.0 + gate_pre * (1.0 - gate_sig))).astype(
        jnp.bfloat16
    )
    grad_normed = lax.psum_scatter(
        (
            jnp.dot(grad_gate, w_gate.T, preferred_element_type=jnp.float32)
            + jnp.dot(grad_up, w_up.T, preferred_element_type=jnp.float32)
        ).astype(jnp.bfloat16),
        "ffn",
        scatter_dimension=0,
        tiled=True,
    ).astype(jnp.float32)
    gained = grad_normed * norm_gain
    inv_cube = inv_rms * inv_rms * inv_rms
    grad_resid = (
        cotangent.astype(jnp.float32)
        + inv_rms * gained
        - hidden_f * inv_cube * jnp.mean(gained * hidden_f, axis=1, keepdims=True)
    ).astype(jnp.bfloat16)
    grad_gain = lax.psum(jnp.sum(grad_normed * hidden_f * inv_rms, axis=0), ("ctx", "ffn"))
    grad_rows = lax.all_gather(grad_resid, "ffn", axis=0, tiled=True)
    grad_attended = jnp.dot(grad_rows, w_out.T, preferred_element_type=jnp.float32).astype(
        jnp.bfloat16
    )
    grad_heads = grad_attended.reshape(row_count, resident_heads, HEAD_WIDTH)
    deltas = jnp.sum(
        grad_heads.astype(jnp.float32)
        * attended_rows.reshape(row_count, resident_heads, HEAD_WIDTH).astype(jnp.float32),
        axis=2,
    )
    delta_heads = deltas.T
    stats_all, deltas_all = (
        lax.all_gather(log_totals.T, "ctx", axis=0, tiled=True),
        lax.all_gather(deltas, "ctx", axis=0, tiled=True),
    )
    shard_rows = lax.all_gather(kv_pair, "ctx", axis=0, tiled=True)
    key_piece = shard_rows[:, 0]
    value_piece = shard_rows[:, 1]
    visible = key_visible(jnp.int32(0), shard_rows.shape[0])

    def update(running):
        scores = (
            jnp.einsum("rhd,kd->hrk", q_heads, key_piece, preferred_element_type=jnp.float32)
            * score_scale
        )
        scores = jnp.where(visible[None], scores, masked_fill)
        prob_weights = jnp.where(visible[None], jnp.exp(scores - log_totals[:, :, None]), 0.0)
        grad_probs = jnp.einsum(
            "rhd,kd->hrk", grad_heads, value_piece, preferred_element_type=jnp.float32
        )
        grad_scores = (prob_weights * (grad_probs - delta_heads[:, :, None])).astype(jnp.bfloat16)
        return (
            jnp.einsum("hrk,kd->rhd", grad_scores, key_piece, preferred_element_type=jnp.float32)
            * score_scale
        )

    grad_query = update(jnp.zeros((row_count, resident_heads, HEAD_WIDTH), jnp.float32))
    zero_block = jnp.zeros((row_count, HEAD_WIDTH), jnp.float32)
    shard_rows = (
        lax.all_gather(queries, "ctx", axis=0, tiled=True),
        lax.all_gather(grad_attended, "ctx", axis=0, tiled=True),
    )
    row_num = shard_rows[0].shape[0]
    q_piece = shard_rows[0].reshape(row_num, resident_heads, HEAD_WIDTH)
    g_piece = shard_rows[1].reshape(row_num, resident_heads, HEAD_WIDTH)
    fold_visible = tile_visible(all_pos, all_seg, positions, own_seg)
    stat_piece = stats_all.T
    delta_piece = deltas_all.T

    def update(running):
        scores = (
            jnp.einsum("qhd,kd->hqk", q_piece, key_own, preferred_element_type=jnp.float32)
            * score_scale
        )
        scores = jnp.where(fold_visible[None], scores, masked_fill)
        prob_weights = jnp.where(fold_visible[None], jnp.exp(scores - stat_piece[:, :, None]), 0.0)
        grad_probs = jnp.einsum(
            "qhd,kd->hqk", g_piece, value_own, preferred_element_type=jnp.float32
        )
        grad_scores = (prob_weights * (grad_probs - delta_piece[:, :, None])).astype(jnp.bfloat16)
        grad_key = (
            jnp.einsum("hqk,qhd->kd", grad_scores, q_piece, preferred_element_type=jnp.float32)
            * score_scale
        )
        grad_value = jnp.einsum(
            "hqk,qhd->kd",
            prob_weights.astype(jnp.bfloat16),
            g_piece,
            preferred_element_type=jnp.float32,
        )
        return (grad_key, grad_value)

    grad_key_own, grad_value_own = update((zero_block, zero_block))
    empty_rows = jnp.zeros((row_count, keys_in.shape[1]), jnp.float32)
    placed_key = lax.dynamic_update_slice_in_dim(
        empty_rows, grad_key_own, key_value_group * HEAD_WIDTH, 1
    )
    placed_value = lax.dynamic_update_slice_in_dim(
        empty_rows, grad_value_own, key_value_group * HEAD_WIDTH, 1
    )
    key_gradient_rows, value_gradient_rows = (
        lax.psum_scatter(
            placed_key.astype(jnp.bfloat16), "ffn", scatter_dimension=0, tiled=True
        ).astype(jnp.float32),
        lax.psum_scatter(
            placed_value.astype(jnp.bfloat16), "ffn", scatter_dimension=0, tiled=True
        ).astype(jnp.float32),
    )
    row_terms = (row_contract(normed_rows, grad_gate), row_contract(normed_rows, grad_up))
    grad_w_gate, grad_w_up = (
        lax.psum_scatter(
            row_terms[0].astype(jnp.bfloat16), "ctx", scatter_dimension=0, tiled=True
        ).astype(jnp.float32),
        lax.psum_scatter(
            row_terms[1].astype(jnp.bfloat16), "ctx", scatter_dimension=0, tiled=True
        ).astype(jnp.float32),
    )
    col_terms = (row_contract(attended_rows, grad_rows), row_contract(activated, cot_rows))
    grad_w_out, grad_w_down = (
        lax.psum_scatter(
            col_terms[0].astype(jnp.bfloat16), "ctx", scatter_dimension=1, tiled=True
        ).astype(jnp.float32),
        lax.psum_scatter(
            col_terms[1].astype(jnp.bfloat16), "ctx", scatter_dimension=1, tiled=True
        ).astype(jnp.float32),
    )
    grad_queries = grad_query.reshape(row_count, resident_heads * HEAD_WIDTH).astype(jnp.bfloat16)
    return (
        mixed,
        grad_resid,
        grad_queries,
        key_gradient_rows,
        value_gradient_rows,
        grad_gain,
        grad_w_out,
        grad_w_gate,
        grad_w_up,
        grad_w_down,
    )


def solution(mesh):
    return jax.shard_map(
        body,
        mesh=mesh,
        in_specs=(
            P(("ctx", "ffn"), None),
            P("ctx", "ffn"),
            P("ctx", None),
            P("ctx", None),
            P("ffn", None),
            P(),
            P(None, "ffn"),
            P(None, "ffn"),
            P("ffn", None),
            P(("ctx", "ffn"), None),
            P("ctx"),
            P(),
        ),
        out_specs=(
            P(("ctx", "ffn"), None),
            P(("ctx", "ffn"), None),
            P("ctx", "ffn"),
            P(("ctx", "ffn"), None),
            P(("ctx", "ffn"), None),
            P(),
            P("ffn", "ctx"),
            P("ctx", "ffn"),
            P("ctx", "ffn"),
            P("ffn", "ctx"),
        ),
        check_vma=False,
    )
```

profile of v0, /device:TPU:32, one launch (start us, length us, event | category | flops | bytes accessed | tf_op | source)
XLA Modules:
  0.0 941.2 jit_solution(1435505484392055501)
XLA Ops:
  9.0 19.0 %all-gather = s32[8,1,128]{2,1,0:T(1,128)S(1)} all-gather(s32[1,1,128]{2,1,0:T(1,128)} %bitcast.186), channel_id=1, replica_groups=mesh['ctx'=8,'ffn'=16] {'ctx'}, dimensions={0}, use_global_device_ids=true | all-gather | bytes 4608 | tf_op jit(solution)/shard_map/all_gather | solution.py:64
  39.2 49.3 %while.21 = (s32[]{:T(128)}, f32[2,128]{1,0:T(2,128)S(1)}, f32[2,128]{1,0:T(2,128)S(1)}, f32[2,128,128]{2,1,0:T(8,128)S(1)}, bf16[128,2,128]{2,0,1:T(8,128)(2,1)...) while((s32[]{:T(128)}, f32[2,128]{1,0:T(2,128)S(1)}, ...), condition=%wide.region_5.6_spmd, body=%wide.region_2.5_spmd.sunk | while | flops 17187348 | bytes 1266056 | solution.py:101
  39.5 6.1 collective-permute-done
  46.5 6.6 collective-permute-done
  54.0 6.1 collective-permute-done
  61.0 6.1 collective-permute-done
  74.9 6.1 collective-permute-done
  81.9 6.1 collective-permute-done
  90.2 66.2 %reduce-scatter.10.cloned.1.call-done = bf16[8,4096]{1,0:T(8,128)(2,1)} async-done(((bf16[128,4096]{1,0:T(8,128)(2,1)}), bf16[8,4096]{1,0:T(8,128)(2,1)}) %reduce-scatter.10.cloned.1.call-update) | async-done | bytes 65552 | tf_op jit(solution)/shard_map/reduce_scatter | solution.py:109
  159.5 43.9 %all-gather.5.cloned.1.call-done = bf16[128,4096]{1,0:T(8,128)(2,1)} async-done(((bf16[8,4096]{1,0:T(8,128)(2,1)}), bf16[128,4096]{1,0:T(8,128)(2,1)}) %all-gather.5.cloned.1.call-update) | async-done | bytes 1048592 | tf_op jit(solution)/shard_map/all_gather | solution.py:119
  209.5 40.0 %all-gather.7.cloned.1.call-done = bf16[128,4096]{1,0:T(8,128)(2,1)} async-done(((bf16[8,4096]{1,0:T(8,128)(2,1)}), bf16[128,4096]{1,0:T(8,128)(2,1)}) %all-gather.7.cloned.1.call-update) | async-done | bytes 1048592 | tf_op jit(solution)/shard_map/all_gather | solution.py:133
  261.7 62.2 %reduce-scatter.14.cloned.1.call-done = bf16[8,4096]{1,0:T(8,128)(2,1)} async-done(((bf16[128,4096]{1,0:T(8,128)(2,1)}), bf16[8,4096]{1,0:T(8,128)(2,1)}) %reduce-scatter.14.cloned.1.call-update) | async-done | bytes 65552 | tf_op jit(solution)/shard_map/reduce_scatter | solution.py:139
  325.9 67.8 %reduce-scatter.12.cloned.1.call-done = bf16[8,4096]{1,0:T(8,128)(2,1)} async-done(((bf16[128,4096]{1,0:T(8,128)(2,1)}), bf16[8,4096]{1,0:T(8,128)(2,1)}) %reduce-scatter.12.cloned.1.call-update) | async-done | bytes 65552 | tf_op jit(solution)/shard_map/reduce_scatter | solution.py:126
  395.5 17.8 %all_gather.33 = f32[1024,2]{0,1:T(2,128)S(1)} all-gather(f32[128,2]{0,1:T(2,128)S(1)} %bitcast.190), channel_id=1, replica_groups=mesh['ctx'=8,'ffn'=16] {'ctx'}, dimensions={0}, use_global_device_ids=true | all-gather | bytes 9216 | tf_op jit(solution)/shard_map/all_gather | solution.py:168
  414.2 24.7 %all_gather.32 = bf16[1024,256]{0,1:T(8,128)(2,1)S(1)} all-gather(bf16[128,256]{0,1:T(8,128)(2,1)S(1)} %copy.44), channel_id=1, replica_groups=mesh['ctx'=8,'ffn'=16] {'ctx'}, dimensions={0}, use_global_device_ids=true | all-gather | bytes 589824 | tf_op jit(solution)/shard_map/all_gather | solution.py:195
  444.1 31.3 %all_gather.34 = bf16[1024,256]{1,0:T(8,128)(2,1)} all-gather(bf16[128,256]{1,0:T(8,128)(2,1)S(1)} %convolution_convert_fusion.6), channel_id=1, replica_groups=mesh['ctx'=8,'ffn'=16] {'ctx'}, dimensions={0}, use_global_device_ids=true | all-gather | bytes 589824 | tf_op jit(solution)/shard_map/all_gather | solution.py:196
  475.4 17.7 %all_gather.35 = f32[1024,2]{0,1:T(2,128)S(1)} all-gather(f32[128,2]{0,1:T(2,128)S(1)} %multiply_reduce_fusion), channel_id=1, replica_groups=mesh['ctx'=8,'ffn'=16] {'ctx'}, dimensions={0}, use_global_device_ids=true | all-gather | bytes 9216 | tf_op jit(solution)/shard_map/all_gather | solution.py:169
  515.1 29.1 %all_gather.30 = bf16[1024,2,128]{2,0,1:T(8,128)(2,1)S(1)} all-gather(bf16[128,2,128]{2,0,1:T(8,128)(2,1)S(1)} %copy-done.17), channel_id=1, replica_groups=mesh['ctx'=8,'ffn'=16] {'ctx'}, dimensions={0}, use_global_device_ids=true | all-gather | bytes 589824 | tf_op jit(solution)/shard_map/all_gather | solution.py:171
  546.2 62.7 %psum.7 = f32[4096]{0:T(1024)} all-reduce(f32[4096]{0:T(1024)S(1)} %copy-done.21), channel_id=1, replica_groups=mesh['ctx'=8,'ffn'=16] {'ctx','ffn'}, use_global_device_ids=true, to_apply=%region_15.16 | all-reduce | flops 4096 | bytes 32768 | tf_op jit(solution)/shard_map/psum | solution.py:155
  612.8 14.5 %reduce-scatter.18.cloned.1.call-done = bf16[8,1024]{1,0:T(8,128)(2,1)} async-done(((bf16[128,1024]{1,0:T(8,128)(2,1)}), bf16[8,1024]{1,0:T(8,128)(2,1)}) %reduce-scatter.18.cloned.1.call-update) | async-done | bytes 16400 | tf_op jit(solution)/shard_map/reduce_scatter | solution.py:240
  628.6 81.0 %reduce-scatter.22.cloned.1.call-done = bf16[512,448]{0,1:T(8,128)(2,1)} async-done(((bf16[4096,448]{0,1:T(8,128)(2,1)}), bf16[512,448]{0,1:T(8,128)(2,1)}) %reduce-scatter.22.cloned.1.call-update) | async-done | bytes 458768 | tf_op jit(solution)/shard_map/reduce_scatter | solution.py:246
  711.7 81.6 %reduce-scatter.24.cloned.1.call-done = bf16[512,448]{0,1:T(8,128)(2,1)} async-done(((bf16[4096,448]{0,1:T(8,128)(2,1)}), bf16[512,448]{0,1:T(8,128)(2,1)}) %reduce-scatter.24.cloned.1.call-update) | async-done | bytes 458768 | tf_op jit(solution)/shard_map/reduce_scatter | solution.py:249
  795.3 81.8 %reduce-scatter.26.cloned.1.call-done = bf16[448,512]{1,0:T(8,128)(2,1)} async-done(((bf16[448,4096]{1,0:T(8,128)(2,1)}), bf16[448,512]{1,0:T(8,128)(2,1)}) %reduce-scatter.26.cloned.1.call-update) | async-done | bytes 458768 | tf_op jit(solution)/shard_map/reduce_scatter | solution.py:258
  879.1 53.4 %reduce-scatter.20.cloned.1.call-done = bf16[256,512]{1,0:T(8,128)(2,1)} async-done(((bf16[256,4096]{1,0:T(8,128)(2,1)}), bf16[256,512]{1,0:T(8,128)(2,1)}) %reduce-scatter.20.cloned.1.call-update) | async-done | bytes 262160 | tf_op jit(solution)/shard_map/reduce_scatter | solution.py:255
  (220 shorter events, 94.4 us)
Async XLA Ops:
  7.2 81.5 %copy-start = (bf16[256,4096]{1,0:T(8,128)(2,1)S(1)}, bf16[256,4096]{1,0:T(8,128)(2,1)}, u32[]{:S(2)}) copy-start(bf16[256,4096]{1,0:T(8,128)(2,1)} %param.18) | copy-start | bytes 6291460
  7.2 149.3 %reduce-scatter.10.cloned.1.call-start = ((), (), s32[]{:S(2)}) async-start(), calls=%async_computation.9 | async-start | bytes 1114112 | tf_op jit(solution)/shard_map/reduce_scatter | solution.py:109
  39.2 6.4 collective-permute-start
  46.1 6.9 collective-permute-start
  53.6 6.4 collective-permute-start
  60.6 6.4 collective-permute-start
  67.6 6.4 collective-permute-start
  74.5 6.4 collective-permute-start
  81.5 6.4 collective-permute-start
  88.5 71.0 %copy-start.24 = (s32[128]{0:T(128)}, s32[128]{0:T(128)S(1)}, u32[]{:S(2)}) copy-start(s32[128]{0:T(128)S(1)} %get-tuple-element.564) | copy-start | bytes 1540
  88.5 324.8 %copy-start.22 = (s32[1024]{0:T(1024)}, s32[1024]{0:T(1024)S(1)}, u32[]{:S(2)}) copy-start(s32[1024]{0:T(1024)S(1)} %get-tuple-element.561) | copy-start | bytes 12292
  90.2 113.2 %all-gather.5.cloned.1.call-start = ((), (), s32[]{:S(2)}) async-start(), calls=%async_computation.10 | async-start | bytes 1114112 | tf_op jit(solution)/shard_map/all_gather | solution.py:119
  158.7 90.8 %all-gather.7.cloned.1.call-start = ((), (), s32[]{:S(2)}) async-start(), calls=%async_computation.12 | async-start | bytes 1114112 | tf_op jit(solution)/shard_map/all_gather | solution.py:133
  159.5 164.4 %reduce-scatter.14.cloned.1.call-start = ((), (), s32[]{:S(2)}) async-start(), calls=%async_computation.13 | async-start | bytes 1114112 | tf_op jit(solution)/shard_map/reduce_scatter | solution.py:139
  257.7 136.0 %copy-start.18 = (bf16[8,4096]{1,0:T(8,128)(2,1)S(1)}, bf16[8,4096]{1,0:T(8,128)(2,1)}, u32[]{:S(2)}) copy-start(bf16[8,4096]{1,0:T(8,128)(2,1)} %param.23) | copy-start | bytes 196612
  257.8 135.9 %reduce-scatter.12.cloned.1.call-start = ((), (), s32[]{:S(2)}) async-start(), calls=%async_computation.11 | async-start | bytes 1114112 | tf_op jit(solution)/shard_map/reduce_scatter | solution.py:126
  261.7 180.3 %all-gather.9.cloned.1.call-start = ((), (), s32[]{:S(2)}) async-start(), calls=%async_computation.14 | async-start | bytes 1114112 | tf_op jit(solution)/shard_map/all_gather | solution.py:156
  395.4 216.1 %reduce-scatter.16.cloned.1.call-start = ((), (), s32[]{:S(2)}) async-start(), calls=%async_computation.15 | async-start | bytes 278528 | tf_op jit(solution)/shard_map/reduce_scatter | solution.py:237
  496.0 131.2 %reduce-scatter.18.cloned.1.call-start = ((), (), s32[]{:S(2)}) async-start(), calls=%async_computation.16 | async-start | bytes 278528 | tf_op jit(solution)/shard_map/reduce_scatter | solution.py:240
  498.5 211.1 %reduce-scatter.22.cloned.1.call-start = ((), (), s32[]{:S(2)}) async-start(), calls=%async_computation.18 | async-start | bytes 4128768 | tf_op jit(solution)/shard_map/reduce_scatter | solution.py:246
  502.6 290.7 %reduce-scatter.24.cloned.1.call-start = ((), (), s32[]{:S(2)}) async-start(), calls=%async_computation.19 | async-start | bytes 4128768 | tf_op jit(solution)/shard_map/reduce_scatter | solution.py:249
  506.4 370.6 %reduce-scatter.26.cloned.1.call-start = ((), (), s32[]{:S(2)}) async-start(), calls=%async_computation.20 | async-start | bytes 4128768 | tf_op jit(solution)/shard_map/reduce_scatter | solution.py:258
  510.7 98.2 %copy-start.15 = (bf16[128,256]{0,1:T(8,128)(2,1)S(1)}, bf16[128,256]{0,1:T(8,128)(2,1)}, u32[]{:S(2)}) copy-start(bf16[128,256]{0,1:T(8,128)(2,1)} %copy-done.14) | copy-start | bytes 196612
  510.7 421.8 %reduce-scatter.20.cloned.1.call-start = ((), (), s32[]{:S(2)}) async-start(), calls=%async_computation.17 | async-start | bytes 2359296 | tf_op jit(solution)/shard_map/reduce_scatter | solution.py:255
  (24 other events, 465.8 us)
Sparse Core Ops, SparseCore 0:
  90.3 66.1 reduce-scatter.9
  159.5 43.8 all-gather.4
  205.9 43.6 all-gather.6
  257.9 65.9 reduce-scatter.13
  327.5 66.1 reduce-scatter.11
  396.6 45.2 all-gather.8
  496.2 62.1 reduce-scatter.15
  562.6 64.6 reduce-scatter.17
  629.7 79.8 reduce-scatter.21
  711.9 81.3 reduce-scatter.23
  795.7 81.3 reduce-scatter.25
  879.3 53.1 reduce-scatter.19
where the time goes:
time: 943 us; the launch traced here: 941 us
  waiting for transfers between devices  636 us (67%)
  blocking collectives  202 us (21%)
  matrix products  46.8 us (5%)
  other arithmetic  20.6 us (2%)
  local copies, waits for them, and re-layouts  18.9 us (2%)
  between operations  14.6 us (2%)
    reduce_scatter x1, waiting for transfers between devices, body(): lax.psum_scatter(col_terms[1].astype(jnp.bfloat16), 'ctx', scatter_dimens...  81.8 us
    reduce_scatter x1, waiting for transfers between devices, body(): lax.psum_scatter(row_terms[1].astype(jnp.bfloat16), 'ctx', scatter_dimens...  81.6 us
    reduce_scatter x1, waiting for transfers between devices, body(): lax.psum_scatter(row_terms[0].astype(jnp.bfloat16), 'ctx', scatter_dimens...  81 us
    reduce_scatter x1, waiting for transfers between devices, body(): lax.psum_scatter(jnp.dot(activated, w_down, preferred_element_type=jnp.fl...  67.8 us
    reduce_scatter x1, waiting for transfers between devices, body(): lax.psum_scatter(jnp.dot(attended_rows, w_out, preferred_element_type=jnp...  66.2 us
    psum x1, blocking collectives, body(): lax.psum(jnp.sum(grad_normed * hidden_f * inv_rms, axis=0), ('ctx', 'ffn'))  62.7 us
    reduce_scatter x1, waiting for transfers between devices, body(): lax.psum_scatter((jnp.dot(grad_gate, w_gate.T, preferred_element_type=jnp...  62.2 us
    reduce_scatter x1, waiting for transfers between devices, body(): lax.psum_scatter(col_terms[0].astype(jnp.bfloat16), 'ctx', scatter_dimens...  53.4 us
  transfers between devices with their start and end apart: 19, of which 17 were waited for; matrix products, arithmetic and copies ran while one was open for 5% of the time, Pallas kernels for 0%

commit v1 on v0

--- a/solution.py
+++ b/solution.py
@@ -9,6 +9,12 @@
 HEAD_WIDTH = 128
 masked_fill = -1e30
 norm_eps = 1e-05
+
+
+def gather_and_add(x, axis):
+    parts = lax.all_gather(x, axis, axis=0, tiled=False)
+    summed = parts.sum(axis=0)
+    return summed
 
 
 def passed_along(value, axis, by):
@@ -152,7 +158,7 @@
         + inv_rms * gained
         - hidden_f * inv_cube * jnp.mean(gained * hidden_f, axis=1, keepdims=True)
     ).astype(jnp.bfloat16)
-    grad_gain = lax.psum(jnp.sum(grad_normed * hidden_f * inv_rms, axis=0), ("ctx", "ffn"))
+    grad_gain = gather_and_add(jnp.sum(grad_normed * hidden_f * inv_rms, axis=0), ("ctx", "ffn"))
     grad_rows = lax.all_gather(grad_resid, "ffn", axis=0, tiled=True)
     grad_attended = jnp.dot(grad_rows, w_out.T, preferred_element_type=jnp.float32).astype(
         jnp.bfloat16

time: 943 us -> 1120 us (1.19)
  waiting for transfers between devices: 636 us -> 874 us
  blocking collectives: 202 us -> 140 us
    all_gather x0 -> x1, waiting for transfers between devices: none -> 196 us  [gather_and_add(): parts = lax.all_gather(x, axis, axis=0, tiled=False)]
    psum x1 -> x0, blocking collectives: 62.7 us -> none  [body(): lax.psum(jnp.sum(grad_normed * hidden_f * inv_rms, axis=0), ('ctx', 'ffn'))]
    reduce_scatter x1, waiting for transfers between devices: 0.01 us -> 60.2 us  [body(): lax.psum_scatter(placed_key.astype(jnp.bfloat16), 'ffn', scatter_dimensio...]
    reduce_scatter x1, waiting for transfers between devices: 14.5 us -> 0.01 us  [body(): lax.psum_scatter(placed_value.astype(jnp.bfloat16), 'ffn', scatter_dimens...]
  transfers between devices with their start and end apart: 19 -> 20, of which waited for: 17 -> 18; matrix products, arithmetic and copies ran while one was open for 5% -> 4% of each run, Pallas kernels for 0% -> 0%
where the time goes in v1:
time: 1120 us
  waiting for transfers between devices  874 us (78%)
  blocking collectives  140 us (12%)
  matrix products  47.4 us (4%)
  other arithmetic  22.2 us (2%)
  local copies, waits for them, and re-layouts  20.2 us (2%)
  between operations  14.3 us (1%)
    all_gather x1, waiting for transfers between devices, gather_and_add(): parts = lax.all_gather(x, axis, axis=0, tiled=False)  196 us
    reduce_scatter x1, waiting for transfers between devices, body(): lax.psum_scatter(row_terms[1].astype(jnp.bfloat16), 'ctx', scatter_dimens...  81.8 us
    reduce_scatter x1, waiting for transfers between devices, body(): lax.psum_scatter(col_terms[1].astype(jnp.bfloat16), 'ctx', scatter_dimens...  81.6 us
    reduce_scatter x1, waiting for transfers between devices, body(): lax.psum_scatter(row_terms[0].astype(jnp.bfloat16), 'ctx', scatter_dimens...  76.9 us
    reduce_scatter x1, waiting for transfers between devices, body(): lax.psum_scatter(jnp.dot(activated, w_down, preferred_element_type=jnp.fl...  67.8 us
    reduce_scatter x1, waiting for transfers between devices, body(): lax.psum_scatter(jnp.dot(attended_rows, w_out, preferred_element_type=jnp...  66.3 us
    reduce_scatter x1, waiting for transfers between devices, body(): lax.psum_scatter((jnp.dot(grad_gate, w_gate.T, preferred_element_type=jnp...  62.2 us
    reduce_scatter x1, waiting for transfers between devices, body(): lax.psum_scatter(placed_key.astype(jnp.bfloat16), 'ffn', scatter_dimensio...  60.2 us
  transfers between devices with their start and end apart: 20, of which 18 were waited for; matrix products, arithmetic and copies ran while one was open for 4% of the time, Pallas kernels for 0%

profile of v1, /device:TPU:32, one launch (start us, length us, event | category | flops | bytes accessed | tf_op | source)
XLA Modules:
  0.0 1119.9 jit_solution(6970376271682859031)
XLA Ops:
  9.5 19.0 %all-gather.1 = s32[8,1,128]{2,1,0:T(1,128)S(1)} all-gather(s32[1,1,128]{2,1,0:T(1,128)} %bitcast.186), channel_id=1, replica_groups=mesh['ctx'=8,'ffn'=16] {'ctx'}, dimensions={0}, use_global_device_ids=true | all-gather | bytes 4608 | tf_op jit(solution)/shard_map/all_gather | solution.py:70
  37.8 49.4 %while.21 = (s32[]{:T(128)}, f32[2,128]{1,0:T(2,128)S(1)}, f32[2,128]{1,0:T(2,128)S(1)}, f32[2,128,128]{2,1,0:T(8,128)S(1)}, bf16[128,2,128]{2,0,1:T(8,128)(2,1)...) while((s32[]{:T(128)}, f32[2,128]{1,0:T(2,128)S(1)}, ...), condition=%wide.region_5.6_spmd, body=%wide.region_2.5_spmd.sunk | while | flops 17187348 | bytes 1266056 | solution.py:107
  38.1 6.1 collective-permute-done
  45.1 6.6 collective-permute-done
  52.6 6.1 collective-permute-done
  59.6 6.1 collective-permute-done
  66.6 6.1 collective-permute-done
  73.5 6.1 collective-permute-done
  88.9 66.3 %reduce-scatter.10.cloned.1.call-done = bf16[8,4096]{1,0:T(8,128)(2,1)} async-done(((bf16[128,4096]{1,0:T(8,128)(2,1)}), bf16[8,4096]{1,0:T(8,128)(2,1)}) %reduce-scatter.10.cloned.1.call-update) | async-done | bytes 65552 | tf_op jit(solution)/shard_map/reduce_scatter | solution.py:115
  158.2 43.8 %all-gather.7.cloned.1.call-done = bf16[128,4096]{1,0:T(8,128)(2,1)} async-done(((bf16[8,4096]{1,0:T(8,128)(2,1)}), bf16[128,4096]{1,0:T(8,128)(2,1)}) %all-gather.7.cloned.1.call-update) | async-done | bytes 1048592 | tf_op jit(solution)/shard_map/all_gather | solution.py:125
  208.2 40.0 %all-gather.9.cloned.1.call-done = bf16[128,4096]{1,0:T(8,128)(2,1)} async-done(((bf16[8,4096]{1,0:T(8,128)(2,1)}), bf16[128,4096]{1,0:T(8,128)(2,1)}) %all-gather.9.cloned.1.call-update) | async-done | bytes 1048592 | tf_op jit(solution)/shard_map/all_gather | solution.py:139
  260.4 62.2 %reduce-scatter.14.cloned.1.call-done = bf16[8,4096]{1,0:T(8,128)(2,1)} async-done(((bf16[128,4096]{1,0:T(8,128)(2,1)}), bf16[8,4096]{1,0:T(8,128)(2,1)}) %reduce-scatter.14.cloned.1.call-update) | async-done | bytes 65552 | tf_op jit(solution)/shard_map/reduce_scatter | solution.py:145
  324.6 67.8 %reduce-scatter.12.cloned.1.call-done = bf16[8,4096]{1,0:T(8,128)(2,1)} async-done(((bf16[128,4096]{1,0:T(8,128)(2,1)}), bf16[8,4096]{1,0:T(8,128)(2,1)}) %reduce-scatter.12.cloned.1.call-update) | async-done | bytes 65552 | tf_op jit(solution)/shard_map/reduce_scatter | solution.py:132
  394.1 17.8 %all_gather.39 = f32[1024,2]{0,1:T(2,128)S(1)} all-gather(f32[128,2]{0,1:T(2,128)S(1)} %bitcast.190), channel_id=1, replica_groups=mesh['ctx'=8,'ffn'=16] {'ctx'}, dimensions={0}, use_global_device_ids=true | all-gather | bytes 9216 | tf_op jit(solution)/shard_map/all_gather | solution.py:174
  412.8 24.7 %all_gather.38 = bf16[1024,256]{0,1:T(8,128)(2,1)S(1)} all-gather(bf16[128,256]{0,1:T(8,128)(2,1)S(1)} %copy.61), channel_id=1, replica_groups=mesh['ctx'=8,'ffn'=16] {'ctx'}, dimensions={0}, use_global_device_ids=true | all-gather | bytes 589824 | tf_op jit(solution)/shard_map/all_gather | solution.py:201
  442.7 31.2 %all_gather.40 = bf16[1024,256]{1,0:T(8,128)(2,1)} all-gather(bf16[128,256]{1,0:T(8,128)(2,1)S(1)} %convolution_convert_fusion.6), channel_id=1, replica_groups=mesh['ctx'=8,'ffn'=16] {'ctx'}, dimensions={0}, use_global_device_ids=true | all-gather | bytes 589824 | tf_op jit(solution)/shard_map/all_gather | solution.py:202
  477.2 17.7 %all_gather.41 = f32[1024,2]{0,1:T(2,128)S(1)} all-gather(f32[128,2]{0,1:T(2,128)S(1)} %multiply_reduce_fusion), channel_id=1, replica_groups=mesh['ctx'=8,'ffn'=16] {'ctx'}, dimensions={0}, use_global_device_ids=true | all-gather | bytes 9216 | tf_op jit(solution)/shard_map/all_gather | solution.py:175
  514.3 29.2 %all_gather.36 = bf16[1024,2,128]{2,0,1:T(8,128)(2,1)S(1)} all-gather(bf16[128,2,128]{2,0,1:T(8,128)(2,1)S(1)} %copy-done.17), channel_id=1, replica_groups=mesh['ctx'=8,'ffn'=16] {'ctx'}, dimensions={0}, use_global_device_ids=true | all-gather | bytes 589824 | tf_op jit(solution)/shard_map/all_gather | solution.py:177
  549.4 60.2 %reduce-scatter.16.cloned.1.call-done = bf16[8,1024]{1,0:T(8,128)(2,1)} async-done(((bf16[128,1024]{1,0:T(8,128)(2,1)}), bf16[8,1024]{1,0:T(8,128)(2,1)}) %reduce-scatter.16.cloned.1.call-update) | async-done | bytes 16400 | tf_op jit(solution)/shard_map/reduce_scatter | solution.py:243
  610.9 195.6 %all-gather.13.cloned.1.call-done = f32[524288]{0:T(1024)} async-done(((f32[4096]{0:T(1024)}), f32[524288]{0:T(1024)}) %all-gather.13.cloned.1.call-update) | async-done | bytes 2097168 | tf_op jit(solution)/shard_map/all_gather | solution.py:15
  811.6 76.9 %reduce-scatter.22.cloned.1.call-done = bf16[512,448]{0,1:T(8,128)(2,1)} async-done(((bf16[4096,448]{0,1:T(8,128)(2,1)}), bf16[512,448]{0,1:T(8,128)(2,1)}) %reduce-scatter.22.cloned.1.call-update) | async-done | bytes 458768 | tf_op jit(solution)/shard_map/reduce_scatter | solution.py:252
  890.5 81.8 %reduce-scatter.24.cloned.1.call-done = bf16[512,448]{0,1:T(8,128)(2,1)} async-done(((bf16[4096,448]{0,1:T(8,128)(2,1)}), bf16[512,448]{0,1:T(8,128)(2,1)}) %reduce-scatter.24.cloned.1.call-update) | async-done | bytes 458768 | tf_op jit(solution)/shard_map/reduce_scatter | solution.py:255
  974.3 81.6 %reduce-scatter.26.cloned.1.call-done = bf16[448,512]{1,0:T(8,128)(2,1)} async-done(((bf16[448,4096]{1,0:T(8,128)(2,1)}), bf16[448,512]{1,0:T(8,128)(2,1)}) %reduce-scatter.26.cloned.1.call-update) | async-done | bytes 458768 | tf_op jit(solution)/shard_map/reduce_scatter | solution.py:264
  1058.0 53.5 %reduce-scatter.20.cloned.1.call-done = bf16[256,512]{1,0:T(8,128)(2,1)} async-done(((bf16[256,4096]{1,0:T(8,128)(2,1)}), bf16[256,512]{1,0:T(8,128)(2,1)}) %reduce-scatter.20.cloned.1.call-update) | async-done | bytes 262160 | tf_op jit(solution)/shard_map/reduce_scatter | solution.py:261
  (226 shorter events, 98.7 us)
Async XLA Ops:
  7.2 80.1 %copy-start = (bf16[256,4096]{1,0:T(8,128)(2,1)S(1)}, bf16[256,4096]{1,0:T(8,128)(2,1)}, u32[]{:S(2)}) copy-start(bf16[256,4096]{1,0:T(8,128)(2,1)} %param.18) | copy-start | bytes 6291460
  7.2 147.9 %reduce-scatter.10.cloned.1.call-start = ((), (), s32[]{:S(2)}) async-start(), calls=%async_computation.9 | async-start | bytes 1114112 | tf_op jit(solution)/shard_map/reduce_scatter | solution.py:115
  37.8 6.4 collective-permute-start
  44.8 6.9 collective-permute-start
  52.2 6.4 collective-permute-start
  59.2 6.4 collective-permute-start
  66.2 6.4 collective-permute-start
  73.2 6.4 collective-permute-start
  80.2 6.4 collective-permute-start
  87.1 71.1 %copy-start.23 = (s32[128]{0:T(128)}, s32[128]{0:T(128)S(1)}, u32[]{:S(2)}) copy-start(s32[128]{0:T(128)S(1)} %get-tuple-element.587) | copy-start | bytes 1540
  87.1 71.1 %copy-start.25 = (s32[1024]{0:T(1024)}, s32[1024]{0:T(1024)S(1)}, u32[]{:S(2)}) copy-start(s32[1024]{0:T(1024)S(1)} %get-tuple-element.588) | copy-start | bytes 12292
  88.8 113.2 %all-gather.7.cloned.1.call-start = ((), (), s32[]{:S(2)}) async-start(), calls=%async_computation.10 | async-start | bytes 1114112 | tf_op jit(solution)/shard_map/all_gather | solution.py:125
  157.4 90.8 %all-gather.9.cloned.1.call-start = ((), (), s32[]{:S(2)}) async-start(), calls=%async_computation.12 | async-start | bytes 1114112 | tf_op jit(solution)/shard_map/all_gather | solution.py:139
  158.1 164.4 %reduce-scatter.14.cloned.1.call-start = ((), (), s32[]{:S(2)}) async-start(), calls=%async_computation.13 | async-start | bytes 1114112 | tf_op jit(solution)/shard_map/reduce_scatter | solution.py:145
  256.4 136.0 %copy-start.18 = (bf16[8,4096]{1,0:T(8,128)(2,1)S(1)}, bf16[8,4096]{1,0:T(8,128)(2,1)}, u32[]{:S(2)}) copy-start(bf16[8,4096]{1,0:T(8,128)(2,1)} %param.23) | copy-start | bytes 196612
  256.4 135.9 %reduce-scatter.12.cloned.1.call-start = ((), (), s32[]{:S(2)}) async-start(), calls=%async_computation.11 | async-start | bytes 1114112 | tf_op jit(solution)/shard_map/reduce_scatter | solution.py:132
  260.3 180.3 %all-gather.11.cloned.1.call-start = ((), (), s32[]{:S(2)}) async-start(), calls=%async_computation.14 | async-start | bytes 1114112 | tf_op jit(solution)/shard_map/all_gather | solution.py:162
  394.0 154.0 %reduce-scatter.18.cloned.1.call-start = ((), (), s32[]{:S(2)}) async-start(), calls=%async_computation.16 | async-start | bytes 278528 | tf_op jit(solution)/shard_map/reduce_scatter | solution.py:246
  477.1 132.5 %reduce-scatter.16.cloned.1.call-start = ((), (), s32[]{:S(2)}) async-start(), calls=%async_computation.15 | async-start | bytes 278528 | tf_op jit(solution)/shard_map/reduce_scatter | solution.py:243
  497.8 308.8 %all-gather.13.cloned.1.call-start = ((), (), s32[]{:S(2)}) async-start(), calls=%async_computation.21 | async-start | bytes 2113536 | tf_op jit(solution)/shard_map/all_gather | solution.py:15
  498.5 389.9 %reduce-scatter.22.cloned.1.call-start = ((), (), s32[]{:S(2)}) async-start(), calls=%async_computation.18 | async-start | bytes 4128768 | tf_op jit(solution)/shard_map/reduce_scatter | solution.py:252
  502.6 469.7 %reduce-scatter.24.cloned.1.call-start = ((), (), s32[]{:S(2)}) async-start(), calls=%async_computation.19 | async-start | bytes 4128768 | tf_op jit(solution)/shard_map/reduce_scatter | solution.py:255
  506.4 549.5 %reduce-scatter.26.cloned.1.call-start = ((), (), s32[]{:S(2)}) async-start(), calls=%async_computation.20 | async-start | bytes 4128768 | tf_op jit(solution)/shard_map/reduce_scatter | solution.py:264
  510.7 600.8 %reduce-scatter.20.cloned.1.call-start = ((), (), s32[]{:S(2)}) async-start(), calls=%async_computation.17 | async-start | bytes 2359296 | tf_op jit(solution)/shard_map/reduce_scatter | solution.py:261
  (26 other events, 428.4 us)
Sparse Core Ops, SparseCore 0:
  88.9 66.1 reduce-scatter.9
  158.2 43.8 all-gather.6
  204.5 43.6 all-gather.8
  256.5 65.9 reduce-scatter.13
  326.1 66.1 reduce-scatter.11
  395.2 45.2 all-gather.10
  477.2 63.4 reduce-scatter.17
  544.9 64.6 reduce-scatter.15
  611.9 194.6 all-gather.12
  808.8 79.6 reduce-scatter.21
  890.9 81.3 reduce-scatter.23
  974.6 81.3 reduce-scatter.25
  1058.3 53.1 reduce-scatter.19
